TPU v7x, 256 devices: a whole 4x4x8 slice. The times are simulated.
256 devices in a mesh: dp: 8 (over y, core), proto: 32 (over z, x).
Axes of the slice: x: 4, y: 4, z: 8, core: 2. Of those that a mesh axis runs over, the one named last changes fastest.
Arguments:
- teacher_features: bfloat16 [6144, 384], P('dp'), may hold values from -8 to 8
- student_features: bfloat16 [6144, 384], P('dp'), may hold values from -8 to 8
- teacher_weight: bfloat16 [384, 131072], P('dp', 'proto'), may hold values from -1 to 1
- student_weight: bfloat16 [384, 131072], P('dp', 'proto'), may hold values from -1 to 1
Outputs:
- teacher_codes: bfloat16 [6144, 131072], P('dp', 'proto')
- head_loss: float32 [], replicated
- weight_grad: float32 [384, 131072], P('dp', 'proto')
All inputs are finite; a program needn't handle non-finite values.
Results may differ from a plain program's by a relative error of at most 0.003.
Values may be sent and summed in bfloat16 or wider, within the bound.
A program may use at most 128 MiB of HBM per device.

v0:
```python
import jax
import jax.numpy as jnp
from jax import lax
from jax.sharding import PartitionSpec as P

ITERS = 3
teacher_temp = 0.07
student_temp = 0.1
norm_eps = 1e-06


def column_norm(weight_rows):
    return jnp.sqrt(jnp.sum(jnp.square(weight_rows.astype(jnp.float32)), axis=0) + norm_eps)


def body(teacher_features, student_features, teacher_weight, student_weight):
    local_crops = teacher_features.shape[0]
    total_crops = local_crops * lax.axis_size("dp")
    total_protos = teacher_weight.shape[1] * lax.axis_size("proto")
    teacher_full, student_full = (
        lax.all_gather(teacher_weight, "dp", axis=0, tiled=True),
        lax.all_gather(student_weight, "dp", axis=0, tiled=True),
    )
    teacher_norm = column_norm(teacher_full)
    student_norm = column_norm(student_full)
    teacher_logits = (
        jnp.dot(teacher_features, teacher_full, preferred_element_type=jnp.float32) / teacher_norm
    )
    student_logits = (
        jnp.dot(student_features, student_full, preferred_element_type=jnp.float32) / student_norm
    )
    teacher_peak, student_peak = lax.pmax(
        (jnp.max(teacher_logits, axis=1), jnp.max(student_logits, axis=1)), "proto"
    )
    powers = jnp.exp((teacher_logits - teacher_peak[:, None]) / teacher_temp)
    shifted = (student_logits - student_peak[:, None]) / student_temp
    student_local = jnp.sum(jnp.exp(shifted), axis=1)
    crop_scale = jnp.ones((local_crops,), jnp.float32)
    for sweep_index in range(ITERS):
        proto_mass = lax.psum(jnp.dot(crop_scale, powers, precision=lax.Precision.HIGHEST), "dp")
        proto_scale = 1.0 / (total_protos * proto_mass)
        crop_local = jnp.dot(powers, proto_scale, precision=lax.Precision.HIGHEST)
        if sweep_index == 0:
            crop_mass = lax.psum(crop_local, "proto")
        else:
            crop_mass = lax.psum(crop_local, "proto")
        crop_scale = 1.0 / (total_crops * crop_mass)
    student_total = lax.psum(student_local, "proto")
    assign = powers * proto_scale[None, :] * crop_scale[:, None] * total_crops
    teacher_codes = assign.astype(jnp.bfloat16)
    log_prob = shifted - jnp.log(student_total)[:, None]
    loss_local = -jnp.sum(assign * log_prob)
    signal = ((jnp.exp(log_prob) - assign) / student_temp).astype(jnp.bfloat16)
    head_loss = lax.psum(loss_local, ("dp", "proto")) / total_crops
    own_weight = student_weight.astype(jnp.float32) / student_norm
    own_grad = lax.psum_scatter(
        lax.dot_general(
            student_features, signal, (((0,), (0,)), ((), ())), preferred_element_type=jnp.float32
        ),
        "dp",
        scatter_dimension=0,
        tiled=True,
    )
    pressure = lax.psum(jnp.sum(own_grad * own_weight, axis=0), "dp")
    weight_grad = (own_grad - own_weight * pressure[None, :]) / student_norm
    return (teacher_codes, head_loss, weight_grad)


def solution(mesh):
    return jax.shard_map(
        body,
        mesh=mesh,
        in_specs=(P("dp", None), P("dp", None), P("dp", "proto"), P("dp", "proto")),
        out_specs=(P("dp", "proto"), P(), P("dp", "proto")),
        check_vma=False,
    )
```

profile of v0, /device:TPU:32, one launch (start us, length us, event | category | flops | bytes accessed | tf_op | source)
XLA Modules:
  0.0 684.9 jit_solution(6292353373318271310)
XLA Ops:
  7.2 0.0 copy-start
  7.2 0.0 all-gather.5.cloned.1.call-start
  7.2 0.7 all-gather.5.cloned.1.call-update
  7.9 0.0 all-gather.3.cloned.1.call-start
  8.0 0.7 all-gather.3.cloned.1.call-update
  8.7 0.0 reduce-scatter.4.cloned.1.call-start
  8.7 34.1 %all-gather.5.cloned.1.call-done = bf16[384,4096]{1,0:T(8,128)(2,1)} async-done(((bf16[48,4096]{1,0:T(8,128)(2,1)}), bf16[384,4096]{1,0:T(8,128)(2,1)}) %all-gather.5.cloned.1.call-update) | async-done | bytes 3145744 | tf_op jit(solution)/shard_map/all_gather | solution.py:22
  42.8 2.6 multiply_reduce_fusion.1
  45.4 29.6 %all-gather.3.cloned.1.call-done = bf16[384,4096]{1,0:T(8,128)(2,1)} async-done(((bf16[48,4096]{1,0:T(8,128)(2,1)}), bf16[384,4096]{1,0:T(8,128)(2,1)}) %all-gather.3.cloned.1.call-update) | async-done | bytes 3145744 | tf_op jit(solution)/shard_map/all_gather | solution.py:21
  75.1 2.6 multiply_reduce_fusion.2
  77.6 0.0 copy-done
  77.7 0.0 copy-start.2
  77.7 0.0 copy-start.4
  77.7 8.5 %fusion.9 = (f32[768]{0:T(1024)S(1)}, f32[768,4096]{1,0:T(8,128)}) fusion(f32[4096]{0:T(1024)S(1)} %add_sqrt_fusion, bf16[768,384]{1,0:T(8,128)(2,1)S(1)} %copy-done, bf16[384,4096]{1,0:T(8,128)(2,1)} %all-gather.5.cloned.1.call-done), kind=kOutput, calls=%fused_computation.33 | convolution fusion | flops 2422209792 | bytes 16337920 | tf_op jit(solution)/shard_map/dot_general | solution.py:30
  86.2 0.0 copy-done.2
  86.2 0.0 copy-done.4
  86.2 6.4 fusion.3
  92.6 70.3 %all-reduce.1 = (f32[768]{0:T(1024)S(1)}, f32[768]{0:T(1024)S(1)}) all-reduce(f32[768]{0:T(1024)S(1)} %get-tuple-element.15, f32[768]{0:T(1024)S(1)} %get-tuple-element.17), channel_id=1, replica_groups=mesh['dp'=8,'proto'=32] {'proto'}, use_global_device_ids=true, to_apply=%region_2.0 | all-reduce | flops 1536 | bytes 12288 | tf_op jit(solution)/shard_map/pmax | solution.py:32
  162.9 10.4 %exponential_reduce_fusion = (f32[768]{0:T(1024)S(1)}, f32[768,4096]{1,0:T(8,128)S(1)}) fusion(f32[768,4096]{1,0:T(8,128)} %get-tuple-element.18, f32[768]{0:T(1024)S(1)} %get-tuple-element.12, f32[768]{0:T(1024)S(1)} %get-tuple-element.11, f32[768,4096]{1,0:T(8,128)} %get-tuple-element.16, f32[4096]{0:T(1024)S(1)} %add_sqrt_fusion.1), kind=kLoop, calls=%fused_computation.2 | loop fusion | flops 18873600 | bytes 37774336 | tf_op jit(solution)/shard_map/reduce_sum | solution.py:37
  173.4 0.0 copy-start.1
  173.4 4.5 copy-done.1
  177.8 6.0 fusion.4
  183.8 24.1 %psum.63 = f32[4096]{0:T(1024)S(1)} all-reduce(f32[4096]{0:T(1024)S(1)} %bitcast.30), channel_id=1, replica_groups=mesh['dp'=8,'proto'=32] {'dp'}, use_global_device_ids=true, to_apply=%region_3.0 | all-reduce | flops 4096 | bytes 32768 | tf_op jit(solution)/shard_map/psum | solution.py:40
  207.9 13.3 %convolution_reduce_fusion.2 = f32[768]{0:T(1024)S(1)} fusion(f32[768,4096]{1,0:T(8,128)} %copy-done.1, f32[4096,1]{0,1:T(1,128)S(1)} %bitcast.26), kind=kOutput, calls=%fused_computation.19 | convolution fusion | flops 37748736 | bytes 12602368 | tf_op jit(solution)/shard_map/dot_general | solution.py:42
  221.2 69.6 %psum.64 = f32[768]{0:T(1024)S(1)} all-reduce(f32[768]{0:T(1024)S(1)} %convolution_reduce_fusion.2), channel_id=1, replica_groups=mesh['dp'=8,'proto'=32] {'proto'}, use_global_device_ids=true, to_apply=%region_4.0 | all-reduce | flops 768 | bytes 6144 | tf_op jit(solution)/shard_map/psum | solution.py:44
  290.9 8.5 %fusion.10 = f32[1,4096]{1,0:T(1,128)S(1)} fusion(f32[768,1]{0,1:T(1,128)S(1)} %reshape.24, f32[768,4096]{1,0:T(8,128)} %copy-done.1), kind=kOutput, calls=%fused_computation.34 | convolution fusion | flops 37748736 | bytes 12602368 | tf_op jit(solution)/shard_map/dot_general | solution.py:40
  299.4 23.6 %psum.65 = f32[4096]{0:T(1024)S(1)} all-reduce(f32[4096]{0:T(1024)S(1)} %bitcast.27), channel_id=1, replica_groups=mesh['dp'=8,'proto'=32] {'dp'}, use_global_device_ids=true, to_apply=%region_5.0 | all-reduce | flops 4096 | bytes 32768 | tf_op jit(solution)/shard_map/psum | solution.py:40
  323.0 13.3 %convolution_reduce_fusion.1 = f32[768]{0:T(1024)S(1)} fusion(f32[768,4096]{1,0:T(8,128)} %copy-done.1, f32[4096,1]{0,1:T(1,128)S(1)} %bitcast.28), kind=kOutput, calls=%fused_computation.18 | convolution fusion | flops 37748736 | bytes 12602368 | tf_op jit(solution)/shard_map/dot_general | solution.py:42
  336.3 71.8 %psum.66 = f32[768]{0:T(1024)S(1)} all-reduce(f32[768]{0:T(1024)S(1)} %convolution_reduce_fusion.1), channel_id=1, replica_groups=mesh['dp'=8,'proto'=32] {'proto'}, use_global_device_ids=true, to_apply=%region_6.0 | all-reduce | flops 768 | bytes 6144 | tf_op jit(solution)/shard_map/psum | solution.py:46
  408.1 8.5 %fusion.11 = f32[1,4096]{1,0:T(1,128)S(1)} fusion(f32[768,1]{0,1:T(1,128)S(1)} %reshape.28, f32[768,4096]{1,0:T(8,128)} %copy-done.1), kind=kOutput, calls=%fused_computation.35 | convolution fusion | flops 37748736 | bytes 12602368 | tf_op jit(solution)/shard_map/dot_general | solution.py:40
  416.6 23.6 %psum.67 = f32[4096]{0:T(1024)S(1)} all-reduce(f32[4096]{0:T(1024)S(1)} %bitcast.29), channel_id=1, replica_groups=mesh['dp'=8,'proto'=32] {'dp'}, use_global_device_ids=true, to_apply=%region_7.0 | all-reduce | flops 4096 | bytes 32768 | tf_op jit(solution)/shard_map/psum | solution.py:40
  440.2 13.3 %convolution_reduce_fusion = f32[768]{0:T(1024)S(1)} fusion(f32[768,4096]{1,0:T(8,128)} %copy-done.1, f32[4096,1]{0,1:T(1,128)S(1)} %bitcast.25), kind=kOutput, calls=%fused_computation.17 | convolution fusion | flops 37748736 | bytes 12602368 | tf_op jit(solution)/shard_map/dot_general | solution.py:42
  453.5 70.9 %all-reduce = (f32[768]{0:T(1024)S(1)}, f32[768]{0:T(1024)S(1)}) all-reduce(f32[768]{0:T(1024)S(1)} %convolution_reduce_fusion, f32[768]{0:T(1024)S(1)} %get-tuple-element.19), channel_id=1, replica_groups=mesh['dp'=8,'proto'=32] {'proto'}, use_global_device_ids=true, to_apply=%region_8.0 | all-reduce | flops 1536 | bytes 12288 | tf_op jit(solution)/shard_map/psum | solution.py:46
  524.4 13.1 %fusion.2 = f32[384,4096]{0,1:T(8,128)} fusion(bf16[768,384]{1,0:T(8,128)(2,1)S(1)} %copy-done, f32[768,4096]{1,0:T(8,128)} %get-tuple-element.18, f32[768,4096]{1,0:T(8,128)} %copy-done.1, f32[768]{0:T(1024)S(1)} %log.3, f32[768]{0:T(1024)S(1)} %get-tuple-element.12, f32[768]{0:T(1024)S(1)} %multiply_divide_fusion.3, f32[4096]{0:T(1024)S(1)} %multiply_divide_fusion), kind=kOutput, calls=%fused_computation.12 | convolution fusion | flops 2444230656 | bytes 32072704 | tf_op jit(solution)/shard_map/dot_general | solution.py:57
  537.5 6.5 copy.11
  544.0 0.0 reduce-scatter.4.cloned.1.call-update
  544.0 0.0 copy-start.3
  544.0 14.4 %multiply_reduce_fusion = (f32[]{:T(128)}, bf16[768,4096]{1,0:T(8,128)(2,1)}) fusion(f32[768,4096]{1,0:T(8,128)} %get-tuple-element.18, f32[768,4096]{1,0:T(8,128)} %copy-done.1, f32[768]{0:T(1024)S(1)} %log.3, f32[768]{0:T(1024)S(1)} %get-tuple-element.12, f32[768]{0:T(1024)S(1)} %multiply_divide_fusion.3, f32[4096]{0:T(1024)S(1)} %multiply_divide_fusion), kind=kLoop, calls=%fused_computation.1 | loop fusion | flops 28311552 | bytes 31482884 | tf_op jit(solution)/shard_map/reduce_sum | solution.py:52
  559.1 0.0 copy-done.3
  559.1 1.3 copy.9
  560.4 80.6 %psum.70 = f32[]{:T(128)} all-reduce(f32[]{:T(128)S(6)} %neg.3), channel_id=1, replica_groups=mesh['dp'=8,'proto'=32] {'dp','proto'}, use_global_device_ids=true, to_apply=%region_15.0 | all-reduce | flops 1 | bytes 8 | tf_op jit(solution)/shard_map/psum | solution.py:54
  641.7 0.0 reduce-scatter.4.cloned.1.call-done
  641.7 1.7 copy.12
  643.4 2.3 multiply_reduce_fusion.3
  645.8 23.6 %psum.71 = f32[4096]{0:T(1024)S(1)} all-reduce(f32[4096]{0:T(1024)S(1)} %multiply_reduce_fusion.3), channel_id=1, replica_groups=mesh['dp'=8,'proto'=32] {'dp'}, use_global_device_ids=true, to_apply=%region_18.0 | all-reduce | flops 4096 | bytes 32768 | tf_op jit(solution)/shard_map/psum | solution.py:64
  669.3 4.6 subtract_divide_fusion
  673.9 3.1 copy.10
  (11 shorter events, 0.1 us)
Async XLA Ops:
  7.2 70.5 %copy-start = (bf16[768,384]{1,0:T(8,128)(2,1)S(1)}, bf16[768,384]{1,0:T(8,128)(2,1)}, u32[]{:S(2)}) copy-start(bf16[768,384]{1,0:T(8,128)(2,1)} %param.5) | copy-start | bytes 1769476
  7.2 35.6 %all-gather.5.cloned.1.call-start = ((), (), s32[]{:S(2)}) async-start(), calls=%async_computation.2 | async-start | bytes 3538944 | tf_op jit(solution)/shard_map/all_gather | solution.py:22
  7.9 67.1 %all-gather.3.cloned.1.call-start = ((), (), s32[]{:S(2)}) async-start(), calls=%async_computation.1 | async-start | bytes 3538944 | tf_op jit(solution)/shard_map/all_gather | solution.py:21
  8.7 633.0 %reduce-scatter.4.cloned.1.call-start = ((), (), s32[]{:S(2)}) async-start(), calls=%async_computation.3 | async-start | bytes 7077888
  77.7 8.6 %copy-start.2 = (bf16[384,4096]{1,0:T(8,128)(2,1)S(1)}, bf16[384,4096]{1,0:T(8,128)(2,1)}, u32[]{:S(2)}) copy-start(bf16[384,4096]{1,0:T(8,128)(2,1)} %all-gather.3.cloned.1.call-done) | copy-start | bytes 9437188
  77.7 8.6 %copy-start.4 = (bf16[768,384]{1,0:T(8,128)(2,1)S(1)}, bf16[768,384]{1,0:T(8,128)(2,1)}, u32[]{:S(2)}) copy-start(bf16[768,384]{1,0:T(8,128)(2,1)} %param.4) | copy-start | bytes 1769476
  173.4 4.5 copy-start.1
  544.0 15.1 %copy-start.3 = (bf16[48,4096]{1,0:T(8,128)(2,1)S(1)}, bf16[48,4096]{1,0:T(8,128)(2,1)}, u32[]{:S(2)}) copy-start(bf16[48,4096]{1,0:T(8,128)(2,1)} %param.7) | copy-start | bytes 1179652
Sparse Core Ops, SparseCore 0:
  9.8 32.9 all-gather.4
  44.6 30.3 all-gather.2
  544.2 46.9 reduce-scatter.3
where the time goes:
time: 689 us; the launch traced here: 685 us
  blocking collectives  458 us (66%)
  matrix products  91 us (13%)
  waiting for transfers between devices  65.2 us (9%)
  other arithmetic  37 us (5%)
  local copies, waits for them, and re-layouts  17.1 us (2%)
  between operations  16.6 us (2%)
    psum x3, blocking collectives, body(): crop_mass = lax.psum(crop_local, 'proto')  212 us
    psum x1, blocking collectives, body(): head_loss = lax.psum(loss_local, ('dp', 'proto')) / total_crops  80.6 us
    psum x3, blocking collectives, body(): lax.psum(jnp.dot(crop_scale, powers, precision=lax.Precision.HIGHEST), 'dp')  71.2 us
    pmax x1, blocking collectives, body(): lax.pmax((jnp.max(teacher_logits, axis=1), jnp.max(student_logits, axis=1...  70.3 us
    dot_general x3, matrix products, body(): crop_local = jnp.dot(powers, proto_scale, precision=lax.Precision.HIGHEST)  39.9 us
    all_gather x1, waiting for transfers between devices, body(): lax.all_gather(student_weight, 'dp', axis=0, tiled=True)  34.1 us
    all_gather x1, waiting for transfers between devices, body(): lax.all_gather(teacher_weight, 'dp', axis=0, tiled=True)  29.6 us
    psum x1, blocking collectives, body(): pressure = lax.psum(jnp.sum(own_grad * own_weight, axis=0), 'dp')  23.6 us
  transfers between devices with their start and end apart: 3, of which 2 were waited for; matrix products, arithmetic and copies ran while one was open for 3% of the time, Pallas kernels for 0%

commit v1 on v0

--- a/solution.py
+++ b/solution.py
@@ -41,7 +41,7 @@
         proto_scale = 1.0 / (total_protos * proto_mass)
         crop_local = jnp.dot(powers, proto_scale, precision=lax.Precision.HIGHEST)
         if sweep_index == 0:
-            crop_mass = lax.psum(crop_local, "proto")
+            crop_mass = jnp.sum(lax.all_gather(crop_local, "proto"), axis=0)
         else:
             crop_mass = lax.psum(crop_local, "proto")
         crop_scale = 1.0 / (total_crops * crop_mass)

time: 689 us -> 660 us (0.958)
  blocking collectives: 458 us -> 429 us
    psum x3 -> x2, blocking collectives: 212 us -> 137 us  [body(): crop_mass = lax.psum(crop_local, 'proto')]
    all_gather x0 -> x1, blocking collectives: none -> 46.5 us  [body(): crop_mass = jnp.sum(lax.all_gather(crop_local, 'proto'), axis=0)]
where the time goes in v1:
time: 660 us; the launch traced here: 656 us
  blocking collectives  429 us (65%)
  matrix products  91 us (14%)
  waiting for transfers between devices  65.2 us (10%)
  other arithmetic  37 us (6%)
  local copies, waits for them, and re-layouts  17.1 us (3%)
  between operations  16.6 us (3%)
    psum x2, blocking collectives, body(): crop_mass = lax.psum(crop_local, 'proto')  137 us
    psum x1, blocking collectives, body(): head_loss = lax.psum(loss_local, ('dp', 'proto')) / total_crops  80.6 us
    psum x3, blocking collectives, body(): lax.psum(jnp.dot(crop_scale, powers, precision=lax.Precision.HIGHEST), 'dp')  71.2 us
    pmax x1, blocking collectives, body(): lax.pmax((jnp.max(teacher_logits, axis=1), jnp.max(student_logits, axis=1...  70.3 us
    all_gather x1, blocking collectives, body(): crop_mass = jnp.sum(lax.all_gather(crop_local, 'proto'), axis=0)  46.5 us
    dot_general x3, matrix products, body(): crop_local = jnp.dot(powers, proto_scale, precision=lax.Precision.HIGHEST)  39.9 us
    all_gather x1, waiting for transfers between devices, body(): lax.all_gather(student_weight, 'dp', axis=0, tiled=True)  34.1 us
    all_gather x1, waiting for transfers between devices, body(): lax.all_gather(teacher_weight, 'dp', axis=0, tiled=True)  29.6 us
  transfers between devices with their start and end apart: 3, of which 2 were waited for; matrix products, arithmetic and copies ran while one was open for 3% of the time, Pallas kernels for 0%

profile of v1, /device:TPU:32, one launch (start us, length us, event | category | flops | bytes accessed | tf_op | source)
XLA Modules:
  0.0 655.7 jit_solution(17613432501952067862)
XLA Ops:
  7.2 0.0 copy-start
  7.2 0.0 all-gather.7.cloned.1.call-start
  7.2 0.7 all-gather.7.cloned.1.call-update
  7.9 0.0 all-gather.5.cloned.1.call-start
  8.0 0.7 all-gather.5.cloned.1.call-update
  8.7 0.0 reduce-scatter.4.cloned.1.call-start
  8.7 34.1 %all-gather.7.cloned.1.call-done = bf16[384,4096]{1,0:T(8,128)(2,1)} async-done(((bf16[48,4096]{1,0:T(8,128)(2,1)}), bf16[384,4096]{1,0:T(8,128)(2,1)}) %all-gather.7.cloned.1.call-update) | async-done | bytes 3145744 | tf_op jit(solution)/shard_map/all_gather | solution.py:22
  42.8 2.6 multiply_reduce_fusion.1
  45.4 29.6 %all-gather.5.cloned.1.call-done = bf16[384,4096]{1,0:T(8,128)(2,1)} async-done(((bf16[48,4096]{1,0:T(8,128)(2,1)}), bf16[384,4096]{1,0:T(8,128)(2,1)}) %all-gather.5.cloned.1.call-update) | async-done | bytes 3145744 | tf_op jit(solution)/shard_map/all_gather | solution.py:21
  75.1 2.6 multiply_reduce_fusion.2
  77.6 0.0 copy-done
  77.7 0.0 copy-start.2
  77.7 0.0 copy-start.4
  77.7 8.5 %fusion.9 = (f32[768]{0:T(1024)S(1)}, f32[768,4096]{1,0:T(8,128)}) fusion(f32[4096]{0:T(1024)S(1)} %add_sqrt_fusion, bf16[768,384]{1,0:T(8,128)(2,1)S(1)} %copy-done, bf16[384,4096]{1,0:T(8,128)(2,1)} %all-gather.7.cloned.1.call-done), kind=kOutput, calls=%fused_computation.33 | convolution fusion | flops 2422209792 | bytes 16337920 | tf_op jit(solution)/shard_map/dot_general | solution.py:30
  86.2 0.0 copy-done.2
  86.2 0.0 copy-done.4
  86.2 6.4 fusion.3
  92.6 70.3 %all-reduce.1 = (f32[768]{0:T(1024)S(1)}, f32[768]{0:T(1024)S(1)}) all-reduce(f32[768]{0:T(1024)S(1)} %get-tuple-element.15, f32[768]{0:T(1024)S(1)} %get-tuple-element.17), channel_id=1, replica_groups=mesh['dp'=8,'proto'=32] {'proto'}, use_global_device_ids=true, to_apply=%region_2.0 | all-reduce | flops 1536 | bytes 12288 | tf_op jit(solution)/shard_map/pmax | solution.py:32
  162.9 10.4 %exponential_reduce_fusion = (f32[768]{0:T(1024)S(1)}, f32[768,4096]{1,0:T(8,128)S(1)}) fusion(f32[768,4096]{1,0:T(8,128)} %get-tuple-element.18, f32[768]{0:T(1024)S(1)} %get-tuple-element.12, f32[768]{0:T(1024)S(1)} %get-tuple-element.11, f32[768,4096]{1,0:T(8,128)} %get-tuple-element.16, f32[4096]{0:T(1024)S(1)} %add_sqrt_fusion.1), kind=kLoop, calls=%fused_computation.2 | loop fusion | flops 18873600 | bytes 37774336 | tf_op jit(solution)/shard_map/reduce_sum | solution.py:37
  173.4 0.0 copy-start.1
  173.4 4.5 copy-done.1
  177.8 6.0 fusion.4
  183.8 24.1 %psum.56 = f32[4096]{0:T(1024)S(1)} all-reduce(f32[4096]{0:T(1024)S(1)} %bitcast.32), channel_id=1, replica_groups=mesh['dp'=8,'proto'=32] {'dp'}, use_global_device_ids=true, to_apply=%region_3.0 | all-reduce | flops 4096 | bytes 32768 | tf_op jit(solution)/shard_map/psum | solution.py:40
  207.9 13.3 %convolution_bitcast_fusion = f32[1,1,768]{2,1,0:T(1,128)S(1)} fusion(f32[768,4096]{1,0:T(8,128)} %copy-done.1, f32[4096,1]{0,1:T(1,128)S(1)} %bitcast.28), kind=kOutput, calls=%fused_computation.19 | convolution fusion | flops 37748736 | bytes 12602368 | tf_op jit(solution)/shard_map/dot_general | solution.py:42
  221.2 46.5 %all-gather.1 = f32[32,1,768]{2,1,0:T(1,128)S(1)} all-gather(f32[1,1,768]{2,1,0:T(1,128)S(1)} %convolution_bitcast_fusion), channel_id=2, replica_groups=mesh['dp'=8,'proto'=32] {'proto'}, dimensions={0}, use_global_device_ids=true | all-gather | bytes 101376 | tf_op jit(solution)/shard_map/all_gather | solution.py:44
  267.6 0.1 reduce_sum.55
  267.7 8.5 %fusion.10 = f32[1,4096]{1,0:T(1,128)S(1)} fusion(f32[768,1]{0,1:T(1,128)S(1)} %reshape.28, f32[768,4096]{1,0:T(8,128)} %copy-done.1), kind=kOutput, calls=%fused_computation.34 | convolution fusion | flops 37748736 | bytes 12602368 | tf_op jit(solution)/shard_map/dot_general | solution.py:40
  276.3 23.6 %psum.57 = f32[4096]{0:T(1024)S(1)} all-reduce(f32[4096]{0:T(1024)S(1)} %bitcast.29), channel_id=1, replica_groups=mesh['dp'=8,'proto'=32] {'dp'}, use_global_device_ids=true, to_apply=%region_5.0 | all-reduce | flops 4096 | bytes 32768 | tf_op jit(solution)/shard_map/psum | solution.py:40
  299.8 13.3 %convolution_reduce_fusion.1 = f32[768]{0:T(1024)S(1)} fusion(f32[768,4096]{1,0:T(8,128)} %copy-done.1, f32[4096,1]{0,1:T(1,128)S(1)} %bitcast.30), kind=kOutput, calls=%fused_computation.18 | convolution fusion | flops 37748736 | bytes 12602368 | tf_op jit(solution)/shard_map/dot_general | solution.py:42
  313.1 65.8 %psum.58 = f32[768]{0:T(1024)S(1)} all-reduce(f32[768]{0:T(1024)S(1)} %convolution_reduce_fusion.1), channel_id=1, replica_groups=mesh['dp'=8,'proto'=32] {'proto'}, use_global_device_ids=true, to_apply=%region_6.0 | all-reduce | flops 768 | bytes 6144 | tf_op jit(solution)/shard_map/psum | solution.py:46
  378.9 8.5 %fusion.11 = f32[1,4096]{1,0:T(1,128)S(1)} fusion(f32[768,1]{0,1:T(1,128)S(1)} %reshape.32, f32[768,4096]{1,0:T(8,128)} %copy-done.1), kind=kOutput, calls=%fused_computation.35 | convolution fusion | flops 37748736 | bytes 12602368 | tf_op jit(solution)/shard_map/dot_general | solution.py:40
  387.5 23.6 %psum.59 = f32[4096]{0:T(1024)S(1)} all-reduce(f32[4096]{0:T(1024)S(1)} %bitcast.31), channel_id=1, replica_groups=mesh['dp'=8,'proto'=32] {'dp'}, use_global_device_ids=true, to_apply=%region_7.0 | all-reduce | flops 4096 | bytes 32768 | tf_op jit(solution)/shard_map/psum | solution.py:40
  411.0 13.3 %convolution_reduce_fusion = f32[768]{0:T(1024)S(1)} fusion(f32[768,4096]{1,0:T(8,128)} %copy-done.1, f32[4096,1]{0,1:T(1,128)S(1)} %bitcast.27), kind=kOutput, calls=%fused_computation.17 | convolution fusion | flops 37748736 | bytes 12602368 | tf_op jit(solution)/shard_map/dot_general | solution.py:42
  424.3 70.9 %all-reduce = (f32[768]{0:T(1024)S(1)}, f32[768]{0:T(1024)S(1)}) all-reduce(f32[768]{0:T(1024)S(1)} %convolution_reduce_fusion, f32[768]{0:T(1024)S(1)} %get-tuple-element.19), channel_id=1, replica_groups=mesh['dp'=8,'proto'=32] {'proto'}, use_global_device_ids=true, to_apply=%region_8.0 | all-reduce | flops 1536 | bytes 12288 | tf_op jit(solution)/shard_map/psum | solution.py:46
  495.2 13.1 %fusion.2 = f32[384,4096]{0,1:T(8,128)} fusion(bf16[768,384]{1,0:T(8,128)(2,1)S(1)} %copy-done, f32[768,4096]{1,0:T(8,128)} %get-tuple-element.18, f32[768,4096]{1,0:T(8,128)} %copy-done.1, f32[768]{0:T(1024)S(1)} %log.3, f32[768]{0:T(1024)S(1)} %get-tuple-element.12, f32[768]{0:T(1024)S(1)} %multiply_divide_fusion.3, f32[4096]{0:T(1024)S(1)} %multiply_divide_fusion), kind=kOutput, calls=%fused_computation.12 | convolution fusion | flops 2444230656 | bytes 32072704 | tf_op jit(solution)/shard_map/dot_general | solution.py:57
  508.3 6.5 copy.11
  514.8 0.0 reduce-scatter.4.cloned.1.call-update
  514.9 0.0 copy-start.3
  514.9 14.4 %multiply_reduce_fusion = (f32[]{:T(128)}, bf16[768,4096]{1,0:T(8,128)(2,1)}) fusion(f32[768,4096]{1,0:T(8,128)} %get-tuple-element.18, f32[768,4096]{1,0:T(8,128)} %copy-done.1, f32[768]{0:T(1024)S(1)} %log.3, f32[768]{0:T(1024)S(1)} %get-tuple-element.12, f32[768]{0:T(1024)S(1)} %multiply_divide_fusion.3, f32[4096]{0:T(1024)S(1)} %multiply_divide_fusion), kind=kLoop, calls=%fused_computation.1 | loop fusion | flops 28311552 | bytes 31482884 | tf_op jit(solution)/shard_map/reduce_sum | solution.py:52
  529.9 0.0 copy-done.3
  529.9 1.3 copy.9
  531.3 80.6 %psum.62 = f32[]{:T(128)} all-reduce(f32[]{:T(128)S(6)} %neg.3), channel_id=1, replica_groups=mesh['dp'=8,'proto'=32] {'dp','proto'}, use_global_device_ids=true, to_apply=%region_15.0 | all-reduce | flops 1 | bytes 8 | tf_op jit(solution)/shard_map/psum | solution.py:54
  612.5 0.0 reduce-scatter.4.cloned.1.call-done
  612.5 1.7 copy.12
  614.2 2.3 multiply_reduce_fusion.3
  616.6 23.6 %psum.63 = f32[4096]{0:T(1024)S(1)} all-reduce(f32[4096]{0:T(1024)S(1)} %multiply_reduce_fusion.3), channel_id=1, replica_groups=mesh['dp'=8,'proto'=32] {'dp'}, use_global_device_ids=true, to_apply=%region_18.0 | all-reduce | flops 4096 | bytes 32768 | tf_op jit(solution)/shard_map/psum | solution.py:64
  640.2 4.6 subtract_divide_fusion
  644.8 3.1 copy.10
  (11 shorter events, 0.1 us)
Async XLA Ops:
  7.2 70.5 %copy-start = (bf16[768,384]{1,0:T(8,128)(2,1)S(1)}, bf16[768,384]{1,0:T(8,128)(2,1)}, u32[]{:S(2)}) copy-start(bf16[768,384]{1,0:T(8,128)(2,1)} %param.5) | copy-start | bytes 1769476
  7.2 35.6 %all-gather.7.cloned.1.call-start = ((), (), s32[]{:S(2)}) async-start(), calls=%async_computation.2 | async-start | bytes 3538944 | tf_op jit(solution)/shard_map/all_gather | solution.py:22
  7.9 67.1 %all-gather.5.cloned.1.call-start = ((), (), s32[]{:S(2)}) async-start(), calls=%async_computation.1 | async-start | bytes 3538944 | tf_op jit(solution)/shard_map/all_gather | solution.py:21
  8.7 603.8 %reduce-scatter.4.cloned.1.call-start = ((), (), s32[]{:S(2)}) async-start(), calls=%async_computation.3 | async-start | bytes 7077888
  77.7 8.6 %copy-start.2 = (bf16[384,4096]{1,0:T(8,128)(2,1)S(1)}, bf16[384,4096]{1,0:T(8,128)(2,1)}, u32[]{:S(2)}) copy-start(bf16[384,4096]{1,0:T(8,128)(2,1)} %all-gather.5.cloned.1.call-done) | copy-start | bytes 9437188
  77.7 8.6 %copy-start.4 = (bf16[768,384]{1,0:T(8,128)(2,1)S(1)}, bf16[768,384]{1,0:T(8,128)(2,1)}, u32[]{:S(2)}) copy-start(bf16[768,384]{1,0:T(8,128)(2,1)} %param.4) | copy-start | bytes 1769476
  173.4 4.5 copy-start.1
  514.9 15.1 %copy-start.3 = (bf16[48,4096]{1,0:T(8,128)(2,1)S(1)}, bf16[48,4096]{1,0:T(8,128)(2,1)}, u32[]{:S(2)}) copy-start(bf16[48,4096]{1,0:T(8,128)(2,1)} %param.7) | copy-start | bytes 1179652
Sparse Core Ops, SparseCore 0:
  9.8 32.9 all-gather.6
  44.6 30.3 all-gather.4
  515.0 46.9 reduce-scatter.3
